TPU v7x, 32 devices: a whole 2x2x4 slice. The times are simulated.
32 devices in a mesh: grp: 4 (over x, core), ep: 8 (over z, y).
Axes of the slice: x: 2, y: 2, z: 4, core: 2. Of those that a mesh axis runs over, the one named last changes fastest.
Arguments:
- features: bfloat16 [8192, 1152], P(('grp', 'ep')), may hold values from -6 to 6
- token_position: int32 [8192], P(('grp', 'ep')), may hold values from 0 to 2047, as said below
- expert_ids: int32 [8192, 2], P(('grp', 'ep')), may hold values from 0 to 7, all different within a row; in each aligned block of 256 rows (0 to 255, 256 to 511, ...) at most 128 rows name the same one
- proj_in: bfloat16 [1152, 2560], P('ep'), may hold values from -0.1875 to 0.1875
- bias_in: float32 [2560], replicated, may hold values from -3 to 3
- proj_out: bfloat16 [2560, 2560], P('ep'), may hold values from -0.125 to 0.125
- bias_out: float32 [2560], replicated, may hold values from -3 to 3
- norm_gain: float32 [2560], replicated, may hold values from 0.1 to 1.9
- router: bfloat16 [2560, 8], replicated, may hold values from -0.125 to 0.125
- w_gate: bfloat16 [8, 2560, 512], P('ep'), may hold values from -0.125 to 0.125
- w_up: bfloat16 [8, 2560, 512], P('ep'), may hold values from -0.125 to 0.125
- w_down: bfloat16 [8, 512, 2560], P('ep'), may hold values from -0.25 to 0.25
Outputs:
- mixed: bfloat16 [8192, 2560], P(('grp', 'ep'))
Inputs may be any that keep to these rules, and one draw needn't show every extreme that they name: `token_position`: within each group of 8 devices along ep, the group's values form a permutation of 0 to 2047; position q belongs to the device of ep index q // 256. The rows of each device hold exactly 32 positions of every device of its group. `expert_ids`: each row names 2 different experts; no expert is named by more than 128 of the rows of one device.
All inputs are finite; a program needn't handle non-finite values.
Results may differ from a plain program's by a relative error of at most 0.0071.
Values may be sent and summed in bfloat16 or wider, within the bound.
A program may use at most 192 MiB of HBM per device.

v0:
```python
import jax
import jax.numpy as jnp
from jax import lax
from jax.sharding import PartitionSpec as P

EPSILON = 1e-06
F32 = jnp.float32
BF16 = jnp.bfloat16


def select_rows(mask, rows):
    return jnp.dot(mask.astype(BF16), rows, preferred_element_type=F32).astype(BF16)


def gather_columns(weight):
    members = lax.axis_size("grp")
    width = weight.shape[1] // members
    part = lax.dynamic_slice_in_dim(weight, lax.axis_index("grp") * width, width, 1)
    full = lax.all_gather(part, ("grp", "ep"), axis=0, tiled=True)
    return full.reshape(members, -1, width)


def shards(
    features,
    token_position,
    expert_ids,
    proj_in,
    bias_in,
    proj_out,
    bias_out,
    norm_gain,
    router,
    w_gate,
    w_up,
    w_down,
):
    members = lax.axis_size("ep")
    row_count, vis = features.shape
    width = proj_in.shape[1]
    first_full = gather_columns(proj_in)
    second_full = gather_columns(proj_out)
    index = jnp.arange(row_count, dtype=jnp.int32)
    rank = jnp.sum((token_position[None, :] < token_position[:, None]).astype(jnp.int32), axis=1)
    local = token_position % row_count
    lane = jnp.arange(128, dtype=jnp.int32)[None, :]
    high, low = ((local // 16)[:, None], (local % 16)[:, None])
    tail = jnp.where(lane == 0, high, jnp.where(lane == 1, low, 0)).astype(BF16)
    order = rank[None, :] == index[:, None]
    sent = select_rows(order, jnp.concatenate([features, tail], axis=1))
    arrived = lax.all_to_all(sent, "ep", split_axis=0, concat_axis=0, tiled=True)
    landing = (arrived[:, vis].astype(F32) * 16 + arrived[:, vis + 1].astype(F32)).astype(jnp.int32)
    patches = select_rows(landing[None, :] == index[:, None], arrived[:, :vis])
    pre_act = jnp.einsum("rk,gkn->rgn", patches, first_full, preferred_element_type=F32)
    pre_act = pre_act.reshape(row_count, width)
    hidden = jax.nn.gelu(pre_act + bias_in, approximate=False).astype(BF16)
    result = jnp.einsum("rk,gkn->rgn", hidden, second_full, preferred_element_type=F32)
    tokens = (result.reshape(row_count, width) + bias_out).astype(BF16)
    wide = tokens.astype(F32)
    scale = lax.rsqrt(jnp.mean(wide * wide, axis=-1, keepdims=True) + EPSILON)
    normed = (wide * scale * norm_gain).astype(BF16)
    experts = router.shape[1]
    top_count = expert_ids.shape[1]
    capacity = 2 * row_count * top_count // experts
    local_experts = w_gate.shape[0]
    logits = jnp.dot(normed, router, preferred_element_type=F32)
    numbers = jnp.arange(experts, dtype=jnp.int32)
    chosen_mask = expert_ids[:, :, None] == numbers[None, None, :]
    chosen = jnp.sum(jnp.where(chosen_mask, logits[:, None, :], 0.0), axis=2)
    first_gate = jax.nn.sigmoid(chosen[:, 0] - chosen[:, 1])
    gates = (first_gate, 1.0 - first_gate)
    named = jnp.any(chosen_mask, axis=1)
    earlier = (index[None, :] < index[:, None]).astype(BF16)
    before = jnp.dot(earlier, named.astype(BF16), preferred_element_type=F32).astype(jnp.int32)
    place = jnp.where(named, before, -1)
    slots = jnp.arange(capacity, dtype=jnp.int32)
    filled = place.T[:, None, :] == slots[None, :, None]
    blocks = select_rows(filled.reshape(experts * capacity, row_count), normed)
    blocks = blocks.reshape(members, local_experts, capacity, width)
    received = lax.all_to_all(blocks, "ep", split_axis=0, concat_axis=0, tiled=True)
    gate_part = jnp.einsum("pecd,edf->pecf", received, w_gate, preferred_element_type=F32)
    up_part = jnp.einsum("pecd,edf->pecf", received, w_up, preferred_element_type=F32)
    activated = (jax.nn.silu(gate_part) * up_part).astype(BF16)
    outputs = jnp.einsum("pecf,efd->pecd", activated, w_down, preferred_element_type=F32).astype(
        BF16
    )
    returned = lax.all_to_all(outputs, "ep", split_axis=0, concat_axis=0, tiled=True)
    returned = returned.reshape(experts * capacity, width)
    total = 0.0
    for choice in range(top_count):
        slot = jnp.where(chosen_mask[:, choice], before, -1)
        picked = (slot[:, :, None] == slots[None, None, :]).reshape(row_count, experts * capacity)
        row = jnp.dot(picked.astype(BF16), returned, preferred_element_type=F32)
        total = total + gates[choice][:, None] * row
    return (wide + total).astype(BF16)


def solution(mesh):
    placed = (
        P(("grp", "ep"), None),
        P(("grp", "ep")),
        P(("grp", "ep"), None),
        P("ep", None),
        P(),
        P("ep", None),
        P(),
        P(),
        P(),
        P("ep", None, None),
        P("ep", None, None),
        P("ep", None, None),
    )
    return jax.shard_map(
        shards, mesh=mesh, in_specs=placed, out_specs=P(("grp", "ep"), None), check_vma=False
    )
```

profile of v0, /device:TPU:0, one launch (start us, length us, event | category | flops | bytes accessed | tf_op | source)
XLA Modules:
  0.0 494.2 jit_solution(15530253404360054965)
XLA Ops:
  6.5 1.8 constant_dynamic-slice_fusion.1
  8.4 1.8 constant_dynamic-slice_fusion
  10.2 0.9 convert_reduce_fusion
  12.0 2.2 convolution_convert_fusion.3
  14.3 7.3 %all-to-all-start = ((bf16[8,32,1280]{2,1,0:T(8,128)(2,1)}), bf16[8,32,1280]{2,1,0:T(8,128)(2,1)S(1)}, u32[]{:S(2)}, u32[]{:S(2)}) async-start(bf16[8,32,1280]{2,1,0:T(8,128)(2,1)} %bitcast.128), calls=%async_computation | async-start | bytes 1310720 | tf_op jit(solution)/shard_map/all_to_all | solution.py:50
  22.6 20.2 %all-to-all-done = bf16[8,32,1280]{2,1,0:T(8,128)(2,1)S(1)} async-done(((bf16[8,32,1280]{2,1,0:T(8,128)(2,1)}), bf16[8,32,1280]{2,1,0:T(8,128)(2,1)S(1)}, u32[]{:S(2)}, u32[]{:S(2)}) %all-to-all-start) | async-done | bytes 655392 | tf_op jit(solution)/shard_map/all_to_all | solution.py:50
  43.5 0.9 copy.43
  44.5 0.9 copy.42
  45.4 1.2 convolution_convert_fusion.2
  46.6 38.9 %all-gather.3.cloned.1.call-done = bf16[4608,640]{1,0:T(8,128)(2,1)} async-done(((bf16[144,640]{1,0:T(8,128)(2,1)}), bf16[4608,640]{1,0:T(8,128)(2,1)}) %all-gather.3.cloned.1.call-update) | async-done | bytes 5898256 | tf_op jit(solution)/shard_map/all_gather | solution.py:19
  85.4 8.9 %copy.36 = bf16[4,640,1152]{2,1,0:T(8,128)(2,1)} copy(bf16[4,640,1152]{1,2,0:T(8,128)(2,1)} %bitcast.124) | data formatting | bytes 11796480 | tf_op jit(solution)/shard_map/rk,gkn->rgn/dot_general | solution.py:53
  94.3 90.3 %all-gather.5.cloned.1.call-done = bf16[10240,640]{1,0:T(8,128)(2,1)} async-done(((bf16[320,640]{1,0:T(8,128)(2,1)}), bf16[10240,640]{1,0:T(8,128)(2,1)}) %all-gather.5.cloned.1.call-update) | async-done | bytes 13107216 | tf_op jit(solution)/shard_map/all_gather | solution.py:19
  184.7 17.7 %copy.37 = bf16[4,640,2560]{2,1,0:T(8,128)(2,1)} copy(bf16[4,640,2560]{1,2,0:T(8,128)(2,1)} %bitcast.122) | data formatting | bytes 26214400 | tf_op jit(solution)/shard_map/rk,gkn->rgn/dot_general | solution.py:56
  202.4 15.8 %fusion.12 = (f32[256]{0:T(256)S(1)}, bf16[256,2560]{1,0:T(8,128)(2,1)}) fusion(f32[2560]{0:T(1024)S(1)} %copy-done.12, bf16[2560,2560]{1,0:T(8,128)(2,1)} %bitcast.123, bf16[256,1152]{1,0:T(8,128)(2,1)S(1)} %copy-done.3, bf16[2560,1152]{1,0:T(8,128)(2,1)} %bitcast.125, f32[2560]{0:T(1024)S(1)} %copy-done.13), kind=kOutput, calls=%fused_computation.21 | convolution fusion | flops 4911923200 | bytes 20927488 | tf_op jit(solution)/shard_map/rk,gkn->rgn/dot_general | solution.py:56
  218.3 3.0 convolution_convert_fusion
  221.2 120.1 %all_to_all.22 = bf16[8,1,128,2560]{3,2,1,0:T(8,128)(2,1)S(1)} all-to-all(bf16[8,1,128,2560]{3,2,1,0:T(8,128)(2,1)S(1)} %bitcast.121), channel_id=1, replica_groups=mesh['grp'=4,'ep'=8] {'ep'}, dimensions={0} | all-to-all | bytes 10485760 | tf_op jit(solution)/shard_map/all_to_all | solution.py:79
  341.4 2.4 copy-done.1
  343.7 4.2 fusion.2
  347.9 10.3 %fusion.4 = bf16[8,1,128,2560]{3,2,1,0:T(8,128)(2,1)} fusion(bf16[1,512,2560]{2,1,0:T(8,128)(2,1)S(1)} %copy-done, bf16[1,2560,512]{2,1,0:T(8,128)(2,1)} %param.22, bf16[8,1,128,2560]{3,2,1,0:T(8,128)(2,1)} %copy-done.1, f32[8,128,512]{2,1,0:T(8,128)} %fusion.2), kind=kOutput, calls=%fused_computation.6 | convolution fusion | flops 5374476288 | bytes 17825792 | tf_op jit(solution)/shard_map/pecf,efd->pecd/dot_general | solution.py:83
  358.3 4.8 all-to-all-start.2
  364.1 1.8 fusion.82
  366.0 112.0 %all-to-all-done.2 = bf16[8,1,128,2560]{3,2,1,0:T(8,128)(2,1)} async-done(((bf16[8,1,128,2560]{3,2,1,0:T(8,128)(2,1)}), bf16[8,1,128,2560]{3,2,1,0:T(8,128)(2,1)}, u32[]{:S(2)}, u32[]{:S(2)}) %all-to-all-start.2) | async-done | bytes 5242912 | tf_op jit(solution)/shard_map/all_to_all | solution.py:86
  478.0 4.1 convolution_multiply_fusion
  482.1 5.2 %fusion.7 = bf16[256,2560]{1,0:T(8,128)(2,1)} fusion(f32[256,2560]{1,0:T(8,128)S(1)} %convolution_multiply_fusion, bf16[1024,2560]{1,0:T(8,128)(2,1)} %bitcast.36, bf16[256,2560]{1,0:T(8,128)(2,1)S(1)} %copy-done.2, f32[256]{0:T(256)S(1)} %bitcast.132, pred[32,8,8,128]{3,2,1,0:T(8,128)(4,1)S(1)} %bitcast.129), kind=kOutput, calls=%fused_computation.16 | convolution fusion | flops 1345454080 | bytes 10748928 | tf_op jit(solution)/shard_map/dot_general | solution.py:92
  (48 shorter events, 3.7 us)
Async XLA Ops:
  6.5 341.4 %copy-start = (bf16[1,512,2560]{2,1,0:T(8,128)(2,1)S(1)}, bf16[1,512,2560]{2,1,0:T(8,128)(2,1)}, u32[]{:S(2)}) copy-start(bf16[1,512,2560]{2,1,0:T(8,128)(2,1)} %param.23) | copy-start | bytes 7864324
  6.5 15.0 %copy-start.7 = (s32[256,2]{0,1:T(2,128)S(1)}, s32[256,2]{0,1:T(2,128)}, u32[]{:S(2)}) copy-start(s32[256,2]{0,1:T(2,128)} %param.14) | copy-start | bytes 6148
  6.5 78.9 %all-gather.3.cloned.1.call-start = ((), (), s32[]{:S(2)}) async-start(), calls=%async_computation.3 | async-start | bytes 6082560 | tf_op jit(solution)/shard_map/all_gather | solution.py:19
  8.4 176.3 %all-gather.5.cloned.1.call-start = ((), (), s32[]{:S(2)}) async-start(), calls=%async_computation.4 | async-start | bytes 13516800 | tf_op jit(solution)/shard_map/all_gather | solution.py:19
  14.3 28.6 %all-to-all-start = ((bf16[8,32,1280]{2,1,0:T(8,128)(2,1)}), bf16[8,32,1280]{2,1,0:T(8,128)(2,1)S(1)}, u32[]{:S(2)}, u32[]{:S(2)}) async-start(bf16[8,32,1280]{2,1,0:T(8,128)(2,1)} %bitcast.128), calls=%async_computation | async-start | bytes 1310720 | tf_op jit(solution)/shard_map/all_to_all | solution.py:50
  184.7 17.7 %copy-start.3 = (bf16[256,1152]{1,0:T(8,128)(2,1)S(1)}, bf16[256,1152]{1,0:T(8,128)(2,1)}, u32[]{:S(2)}) copy-start(bf16[256,1152]{1,0:T(8,128)(2,1)} %convolution_convert_fusion.2) | copy-start | bytes 1769476
  184.7 17.7 %copy-start.12 = (f32[2560]{0:T(1024)S(1)}, f32[2560]{0:T(1024)}, u32[]{:S(2)}) copy-start(f32[2560]{0:T(1024)} %param.18) | copy-start | bytes 30724
  184.7 17.7 %copy-start.13 = (f32[2560]{0:T(1024)S(1)}, f32[2560]{0:T(1024)}, u32[]{:S(2)}) copy-start(f32[2560]{0:T(1024)} %param.16) | copy-start | bytes 30724
  202.4 15.9 %copy-start.4 = (f32[2560]{0:T(1024)S(1)}, f32[2560]{0:T(1024)}, u32[]{:S(2)}) copy-start(f32[2560]{0:T(1024)} %param.19) | copy-start | bytes 30724
  218.2 3.0 copy-start.8
  221.2 122.5 %copy-start.10 = (bf16[1,2560,512]{2,1,0:T(8,128)(2,1)S(1)}, bf16[1,2560,512]{2,1,0:T(8,128)(2,1)}, u32[]{:S(2)}) copy-start(bf16[1,2560,512]{2,1,0:T(8,128)(2,1)} %param.21) | copy-start | bytes 7864324
  341.4 2.4 copy-start.1
  358.3 4.8 copy-start.6
  358.3 5.0 %copy-start.5 = (s32[256,8]{0,1:T(8,128)S(1)}, s32[256,8]{0,1:T(8,128)}, u32[]{:S(2)}) copy-start(s32[256,8]{0,1:T(8,128)} %get-tuple-element.11) | copy-start | bytes 24580
  358.3 5.8 %copy-start.9 = (f32[256]{0:T(256)S(1)}, f32[256]{0:T(256)}, u32[]{:S(2)}) copy-start(f32[256]{0:T(256)} %copy-done.8) | copy-start | bytes 3076
  358.3 5.8 %copy-start.11 = (bf16[2560,8]{0,1:T(8,128)(2,1)S(1)}, bf16[2560,8]{0,1:T(8,128)(2,1)}, u32[]{:S(2)}) copy-start(bf16[2560,8]{0,1:T(8,128)(2,1)} %param.20) | copy-start | bytes 122884
  358.3 119.7 %all-to-all-start.2 = ((bf16[8,1,128,2560]{3,2,1,0:T(8,128)(2,1)}), bf16[8,1,128,2560]{3,2,1,0:T(8,128)(2,1)}, u32[]{:S(2)}, u32[]{:S(2)}) async-start(bf16[8,1,128,2560]{3,2,1,0:T(8,128)(2,1)} %fusion.4), calls=%async_computation.2 | async-start | bytes 10485760 | tf_op jit(solution)/shard_map/all_to_all | solution.py:86
  478.0 4.1 copy-start.2
Sparse Core Ops, SparseCore 0:
  10.2 75.1 all-gather.2
  88.3 96.3 all-gather.4
where the time goes:
time: 496 us; the launch traced here: 494 us
  waiting for transfers between devices  261 us (53%)
  blocking collectives  120 us (24%)
  matrix products  48.7 us (10%)
  local copies, waits for them, and re-layouts  35.4 us (7%)
  between operations  13.6 us (3%)
  starting transfers between devices  12.2 us (2%)
    all_gather x2, waiting for transfers between devices, gather_columns(): full = lax.all_gather(part, ('grp', 'ep'), axis=0, tiled=True)  129 us
    all_to_all x1, blocking collectives, shards(): lax.all_to_all(blocks, 'ep', split_axis=0, concat_axis=0, tiled=True)  120 us
    all_to_all x1, waiting for transfers between devices, shards(): lax.all_to_all(outputs, 'ep', split_axis=0, concat_axis=0, tiled=True)  112 us
    all_to_all x1, waiting for transfers between devices, shards(): lax.all_to_all(sent, 'ep', split_axis=0, concat_axis=0, tiled=True)  20.2 us
    dot_general x1, local copies, waits for them, and re-layouts, shards(): jnp.einsum('rk,gkn->rgn', hidden, second_full, preferred_element_type=F32)  17.7 us
    dot_general x1, matrix products, shards(): jnp.einsum('rk,gkn->rgn', hidden, second_full, preferred_element_type=F32)  15.8 us
    dot_general x1, matrix products, shards(): jnp.einsum('pecf,efd->pecd', activated, w_down, preferred_element_type=F32)  10.3 us
  transfers between devices with their start and end apart: 4, of which 4 were waited for; matrix products, arithmetic and copies ran while one was open for 5% of the time, Pallas kernels for 0%

commit v1 on v0

--- a/solution.py
+++ b/solution.py
@@ -16,7 +16,8 @@
     members = lax.axis_size("grp")
     width = weight.shape[1] // members
     part = lax.dynamic_slice_in_dim(weight, lax.axis_index("grp") * width, width, 1)
-    full = lax.all_gather(part, ("grp", "ep"), axis=0, tiled=True)
+    outgoing = jnp.stack([part] * lax.axis_size(("grp", "ep")))
+    full = jnp.concatenate(lax.all_to_all(outgoing, ("grp", "ep"), 0, 0), axis=0)
     return full.reshape(members, -1, width)
 
 

time: 496 us -> 777 us (1.57)
  waiting for transfers between devices: 261 us -> 540 us
  between operations: 13.6 us -> 0.23 us
  local copies, waits for them, and re-layouts: 35.4 us -> 45 us
    all_to_all x0 -> x2, waiting for transfers between devices: none -> 412 us  [gather_columns(): lax.all_to_all(outgoing, ('grp', 'ep'), 0, 0)]
    all_gather x2 -> x0, waiting for transfers between devices: 129 us -> none  [gather_columns(): full = lax.all_gather(part, ('grp', 'ep'), axis=0, tiled=True)]
    another operation x0 -> x2, local copies, waits for them, and re-layouts: none -> 10.5 us  [gather_columns(): outgoing = jnp.stack([part] * lax.axis_size(('grp', 'ep')))]
  transfers between devices with their start and end apart: 4 -> 4, of which waited for: 4 -> 4; matrix products, arithmetic and copies ran while one was open for 5% -> 2% of each run, Pallas kernels for 0% -> 0%
where the time goes in v1:
time: 777 us; the launch traced here: 776 us
  waiting for transfers between devices  540 us (69%)
  blocking collectives  118 us (15%)
  matrix products  48.7 us (6%)
  local copies, waits for them, and re-layouts  45 us (6%)
  starting transfers between devices  19.8 us (3%)
    all_to_all x2, waiting for transfers between devices, gather_columns(): lax.all_to_all(outgoing, ('grp', 'ep'), 0, 0)  412 us
    all_to_all x1, blocking collectives, shards(): lax.all_to_all(blocks, 'ep', split_axis=0, concat_axis=0, tiled=True)  118 us
    all_to_all x1, waiting for transfers between devices, shards(): lax.all_to_all(outputs, 'ep', split_axis=0, concat_axis=0, tiled=True)  112 us
    dot_general x1, local copies, waits for them, and re-layouts, shards(): jnp.einsum('rk,gkn->rgn', hidden, second_full, preferred_element_type=F32)  17.7 us
    all_to_all x1, waiting for transfers between devices, shards(): lax.all_to_all(sent, 'ep', split_axis=0, concat_axis=0, tiled=True)  16.4 us
    dot_general x1, matrix products, shards(): jnp.einsum('rk,gkn->rgn', hidden, second_full, preferred_element_type=F32)  15.9 us
  transfers between devices with their start and end apart: 4, of which 4 were waited for; matrix products, arithmetic and copies ran while one was open for 2% of the time, Pallas kernels for 0%

profile of v1, /device:TPU:0, one launch (start us, length us, event | category | flops | bytes accessed | tf_op | source)
XLA Modules:
  0.0 775.5 jit_solution(17703631027830720854)
XLA Ops:
  1.9 2.3 convolution_convert_fusion.3
  4.2 7.3 all-to-all-start
  12.4 16.4 %all-to-all-done = bf16[8,32,1280]{2,1,0:T(8,128)(2,1)S(1)} async-done(((bf16[8,32,1280]{2,1,0:T(8,128)(2,1)}), bf16[8,32,1280]{2,1,0:T(8,128)(2,1)S(1)}, u32[]{:S(2)}, u32[]{:S(2)}) %all-to-all-start) | async-done | bytes 655392 | tf_op jit(solution)/shard_map/all_to_all | solution.py:51
  28.8 3.0 stack.4
  31.8 3.8 all-to-all-start.1
  35.5 1.8 constant_dynamic-slice_fusion
  37.3 131.9 %all-to-all-done.1 = bf16[32,144,640]{2,1,0:T(8,128)(2,1)} async-done(((bf16[32,144,640]{2,1,0:T(8,128)(2,1)}), bf16[32,144,640]{2,1,0:T(8,128)(2,1)}, u32[]{:S(2)}, u32[]{:S(2)}) %all-to-all-start.1) | async-done | bytes 5898272 | tf_op jit(solution)/shard_map/all_to_all | solution.py:20
  169.3 7.5 stack.5
  176.8 3.9 all-to-all-start.2
  184.3 1.2 convolution_convert_fusion.2
  185.5 8.9 %copy.36 = bf16[4,640,1152]{2,1,0:T(8,128)(2,1)} copy(bf16[4,640,1152]{1,2,0:T(8,128)(2,1)} %bitcast.4) | data formatting | bytes 11796480 | tf_op jit(solution)/shard_map/rk,gkn->rgn/dot_general | solution.py:54
  194.4 280.3 %all-to-all-done.2 = bf16[32,320,640]{2,1,0:T(8,128)(2,1)} async-done(((bf16[32,320,640]{2,1,0:T(8,128)(2,1)}), bf16[32,320,640]{2,1,0:T(8,128)(2,1)}, u32[]{:S(2)}, u32[]{:S(2)}) %all-to-all-start.2) | async-done | bytes 13107232 | tf_op jit(solution)/shard_map/all_to_all | solution.py:20
  474.7 17.7 %copy.37 = bf16[4,640,2560]{2,1,0:T(8,128)(2,1)} copy(bf16[4,640,2560]{1,2,0:T(8,128)(2,1)} %bitcast.7) | data formatting | bytes 26214400 | tf_op jit(solution)/shard_map/rk,gkn->rgn/dot_general | solution.py:57
  492.4 15.9 %fusion.12 = (f32[256]{0:T(256)S(1)}, bf16[256,2560]{1,0:T(8,128)(2,1)}) fusion(f32[2560]{0:T(1024)S(1)} %copy-done.12, bf16[2560,2560]{1,0:T(8,128)(2,1)} %bitcast.122, bf16[256,1152]{1,0:T(8,128)(2,1)S(1)} %copy-done.3, bf16[2560,1152]{1,0:T(8,128)(2,1)} %bitcast.123, f32[2560]{0:T(1024)S(1)} %copy-done.13), kind=kOutput, calls=%fused_computation.21 | convolution fusion | flops 4911923200 | bytes 20927488 | tf_op jit(solution)/shard_map/rk,gkn->rgn/dot_general | solution.py:57
  508.2 3.0 convolution_convert_fusion
  511.2 118.5 %all_to_all.32 = bf16[8,1,128,2560]{3,2,1,0:T(8,128)(2,1)S(1)} all-to-all(bf16[8,1,128,2560]{3,2,1,0:T(8,128)(2,1)S(1)} %bitcast.121), channel_id=1, replica_groups=mesh['grp'=4,'ep'=8] {'ep'}, dimensions={0} | all-to-all | bytes 10485760 | tf_op jit(solution)/shard_map/all_to_all | solution.py:80
  629.7 2.3 copy-done.1
  632.0 4.2 fusion.2
  636.2 10.3 %fusion.4 = bf16[8,1,128,2560]{3,2,1,0:T(8,128)(2,1)} fusion(bf16[1,512,2560]{2,1,0:T(8,128)(2,1)S(1)} %copy-done, bf16[1,2560,512]{2,1,0:T(8,128)(2,1)} %param.22, bf16[8,1,128,2560]{3,2,1,0:T(8,128)(2,1)} %copy-done.1, f32[8,128,512]{2,1,0:T(8,128)} %fusion.2), kind=kOutput, calls=%fused_computation.6 | convolution fusion | flops 5374476288 | bytes 17825792 | tf_op jit(solution)/shard_map/pecf,efd->pecd/dot_general | solution.py:84
  646.6 4.8 all-to-all-start.4
  652.4 1.8 fusion.82
  654.3 111.9 %all-to-all-done.4 = bf16[8,1,128,2560]{3,2,1,0:T(8,128)(2,1)} async-done(((bf16[8,1,128,2560]{3,2,1,0:T(8,128)(2,1)}), bf16[8,1,128,2560]{3,2,1,0:T(8,128)(2,1)}, u32[]{:S(2)}, u32[]{:S(2)}) %all-to-all-start.4) | async-done | bytes 5242912 | tf_op jit(solution)/shard_map/all_to_all | solution.py:87
  766.2 4.1 convolution_multiply_fusion
  770.3 5.2 fusion.7
  (48 shorter events, 7.5 us)
Async XLA Ops:
  0.0 636.2 %copy-start = (bf16[1,512,2560]{2,1,0:T(8,128)(2,1)S(1)}, bf16[1,512,2560]{2,1,0:T(8,128)(2,1)}, u32[]{:S(2)}) copy-start(bf16[1,512,2560]{2,1,0:T(8,128)(2,1)} %param.23) | copy-start | bytes 7864324
  4.2 24.6 %all-to-all-start = ((bf16[8,32,1280]{2,1,0:T(8,128)(2,1)}), bf16[8,32,1280]{2,1,0:T(8,128)(2,1)S(1)}, u32[]{:S(2)}, u32[]{:S(2)}) async-start(bf16[8,32,1280]{2,1,0:T(8,128)(2,1)} %bitcast.126), calls=%async_computation | async-start | bytes 1310720 | tf_op jit(solution)/shard_map/all_to_all | solution.py:51
  31.8 137.5 %all-to-all-start.1 = ((bf16[32,144,640]{2,1,0:T(8,128)(2,1)}), bf16[32,144,640]{2,1,0:T(8,128)(2,1)}, u32[]{:S(2)}, u32[]{:S(2)}) async-start(bf16[32,144,640]{2,1,0:T(8,128)(2,1)} %stack.4), calls=%async_computation.1 | async-start | bytes 11796480 | tf_op jit(solution)/shard_map/all_to_all | solution.py:20
  176.8 3.9 copy-start.7
  176.8 297.9 %all-to-all-start.2 = ((bf16[32,320,640]{2,1,0:T(8,128)(2,1)}), bf16[32,320,640]{2,1,0:T(8,128)(2,1)}, u32[]{:S(2)}, u32[]{:S(2)}) async-start(bf16[32,320,640]{2,1,0:T(8,128)(2,1)} %stack.5), calls=%async_computation.2 | async-start | bytes 26214400 | tf_op jit(solution)/shard_map/all_to_all | solution.py:20
  474.7 17.7 %copy-start.3 = (bf16[256,1152]{1,0:T(8,128)(2,1)S(1)}, bf16[256,1152]{1,0:T(8,128)(2,1)}, u32[]{:S(2)}) copy-start(bf16[256,1152]{1,0:T(8,128)(2,1)} %convolution_convert_fusion.2) | copy-start | bytes 1769476
  474.7 17.7 %copy-start.12 = (f32[2560]{0:T(1024)S(1)}, f32[2560]{0:T(1024)}, u32[]{:S(2)}) copy-start(f32[2560]{0:T(1024)} %param.18) | copy-start | bytes 30724
  474.7 17.7 %copy-start.13 = (f32[2560]{0:T(1024)S(1)}, f32[2560]{0:T(1024)}, u32[]{:S(2)}) copy-start(f32[2560]{0:T(1024)} %param.16) | copy-start | bytes 30724
  492.3 15.9 %copy-start.4 = (f32[2560]{0:T(1024)S(1)}, f32[2560]{0:T(1024)}, u32[]{:S(2)}) copy-start(f32[2560]{0:T(1024)} %param.19) | copy-start | bytes 30724
  508.2 3.0 copy-start.8
  511.2 120.8 %copy-start.10 = (bf16[1,2560,512]{2,1,0:T(8,128)(2,1)S(1)}, bf16[1,2560,512]{2,1,0:T(8,128)(2,1)}, u32[]{:S(2)}) copy-start(bf16[1,2560,512]{2,1,0:T(8,128)(2,1)} %param.21) | copy-start | bytes 7864324
  629.7 2.4 copy-start.1
  646.6 4.9 copy-start.6
  646.6 5.0 copy-start.5
  646.6 5.8 copy-start.9
  646.6 5.8 copy-start.11
  646.6 119.6 %all-to-all-start.4 = ((bf16[8,1,128,2560]{3,2,1,0:T(8,128)(2,1)}), bf16[8,1,128,2560]{3,2,1,0:T(8,128)(2,1)}, u32[]{:S(2)}, u32[]{:S(2)}) async-start(bf16[8,1,128,2560]{3,2,1,0:T(8,128)(2,1)} %fusion.4), calls=%async_computation.4 | async-start | bytes 10485760 | tf_op jit(solution)/shard_map/all_to_all | solution.py:87
  766.2 4.1 copy-start.2
